TPU v7x, 128 devices: a whole 4x4x4 slice. The times are simulated.
128 devices in a mesh: row: 4 (over y_hi, core), col: 32 (over x, z, y_lo).
Axes of the slice: x: 4, y: 4 (y_hi: 2, y_lo: 2; y = y_hi * 2 + y_lo), z: 4, core: 2. Of those that a mesh axis runs over, the one named last changes fastest.
Arguments:
- inputs: bfloat16 [1024, 8192], P(('row', 'col')), may hold values from -6 to 6
- layer_norm_gain: float32 [8192], replicated, may hold values from 0.1 to 1.9
- w_in: bfloat16 [8192, 16384], P('row', 'col'), may hold values from -0.09375 to 0.09375
- w_out: bfloat16 [16384, 8192], P('col', 'row'), may hold values from -0.0625 to 0.0625
- pattern_in: int32 [64, 16], replicated, may hold values from 0 to 31, as said below
- pattern_out: int32 [32, 32], replicated, may hold values from 0 to 63, as said below
- out_grad: bfloat16 [1024, 8192], P(('row', 'col')), may hold values from -6 to 6
Outputs:
- output: bfloat16 [1024, 8192], P(('row', 'col'))
- grad_inputs: bfloat16 [1024, 8192], P(('row', 'col'))
- grad_w_in: bfloat16 [8192, 16384], P('row', 'col')
- grad_w_out: bfloat16 [16384, 8192], P('col', 'row')
- norm_gain_gradient: float32 [8192], replicated
Inputs may be any that keep to these rules, and one draw needn't show every extreme that they name: `pattern_in`: each row lists 8192 / 512 different tile rows in increasing order. `pattern_out`: each row lists 16384 / 512 different tile rows in increasing order.
All inputs are finite; a program needn't handle non-finite values.
Results may differ from a plain program's by a relative error of at most 0.022.
Values may be sent and summed in bfloat16 or wider, within the bound.
A program may use at most 128 MiB of HBM per device.

v0:
```python
import jax
import jax.numpy as jnp
from jax import lax
from jax.sharding import PartitionSpec as P

D = 8192
FF = 16384
BLOCK = 256


def cut_along(shard, dim, count):
    before, after = (shard.shape[:dim], shard.shape[dim + 1 :])
    return jnp.moveaxis(shard.reshape(*before, count, -1, *after), dim, 0)


def sum_at_owner(shard, axis, dim):
    pieces = cut_along(shard, dim, lax.axis_size(axis))
    arrived = lax.all_to_all(pieces, axis, split_axis=0, concat_axis=0, tiled=True)
    return arrived.astype(jnp.float32).sum(axis=0)


def block_mask(pattern, tile_rows):
    iota = jnp.arange(tile_rows, dtype=jnp.int32)
    return jnp.any(pattern[None, :, :] == iota[:, None, None], axis=2)


def apply_mask(weight, mask):
    rows_t, cols_t = mask.shape
    shaped = weight.reshape(rows_t, BLOCK, cols_t, BLOCK)
    kept = jnp.where(mask[:, None, :, None], shaped, jnp.zeros((), weight.dtype))
    return kept.reshape(weight.shape)


def gelu_value(h):
    inner = 0.7978845608 * (h + 0.044715 * h * h * h)
    return 0.5 * h * (1.0 + jnp.tanh(inner))


def gelu_slope(h):
    tanh_v = jnp.tanh(0.7978845608 * (h + 0.044715 * h * h * h))
    return 0.5 * (1.0 + tanh_v) + 0.5 * h * (1.0 - tanh_v * tanh_v) * 0.7978845608 * (
        1.0 + 0.134145 * h * h
    )


def dot_last(left, right):
    return lax.dot_general(
        left, right, (((1,), (1,)), ((), ())), preferred_element_type=jnp.float32
    )


def dot_first(left, right):
    return lax.dot_general(
        left, right, (((0,), (0,)), ((), ())), preferred_element_type=jnp.float32
    )


def shards(inputs, layer_norm_gain, w_in, w_out, pattern_in, pattern_out, out_grad):
    n_row = lax.axis_size("row")
    n_col = lax.axis_size("col")
    row_index = lax.axis_index("row")
    col_index = lax.axis_index("col")
    tok_here = inputs.shape[0]
    feat_tiles = w_in.shape[0] // BLOCK
    unit_tiles = w_in.shape[1] // BLOCK
    mask_in = lax.dynamic_slice(
        block_mask(pattern_in, D // BLOCK),
        (row_index * feat_tiles, col_index * unit_tiles),
        (feat_tiles, unit_tiles),
    )
    mask_out = lax.dynamic_slice(
        block_mask(pattern_out, FF // BLOCK),
        (col_index * unit_tiles, row_index * feat_tiles),
        (unit_tiles, feat_tiles),
    )
    w_in_e = apply_mask(w_in, mask_in)
    w_out_e = apply_mask(w_out, mask_out)
    xfloat = inputs.astype(jnp.float32)
    centered_input = xfloat - jnp.mean(xfloat, axis=1, keepdims=True)
    inverse_deviation = lax.rsqrt(
        jnp.mean(centered_input * centered_input, axis=1, keepdims=True) + 1e-05
    )
    standardized_input = centered_input * inverse_deviation
    normalized_input = (standardized_input * layer_norm_gain[None, :]).astype(jnp.bfloat16)
    swapped = lax.all_to_all(normalized_input, "row", split_axis=1, concat_axis=0, tiled=True)
    allrows = lax.all_gather(swapped, "col", axis=0, tiled=True)
    slice_width = allrows.shape[1]
    byrow = (
        allrows.reshape(n_col, n_row, tok_here, slice_width)
        .transpose(1, 0, 2, 3)
        .reshape(-1, slice_width)
    )
    hidden_pre = lax.psum_scatter(
        jnp.dot(byrow, w_in_e, preferred_element_type=jnp.float32).astype(jnp.bfloat16),
        "row",
        scatter_dimension=0,
        tiled=True,
    ).astype(jnp.float32)
    activation = gelu_value(hidden_pre).astype(jnp.bfloat16)
    w_out_full = lax.all_gather(w_out_e, "row", axis=1, tiled=True)
    summed = sum_at_owner(
        jnp.dot(activation, w_out_full, preferred_element_type=jnp.float32).astype(jnp.bfloat16),
        "col",
        0,
    )
    output = (xfloat + summed).astype(jnp.bfloat16)
    grad_panel = lax.all_gather(out_grad, "col", axis=0, tiled=True)
    d_act = dot_last(grad_panel, w_out_full)
    d_pre = (d_act * gelu_slope(hidden_pre)).astype(jnp.bfloat16)
    w2_sum = lax.psum_scatter(
        dot_first(activation, grad_panel).astype(jnp.bfloat16),
        "row",
        scatter_dimension=1,
        tiled=True,
    )
    grad_w_out = apply_mask(w2_sum, mask_out)
    d_all = lax.all_gather(d_pre, "row", axis=0, tiled=True)
    unit_width = d_all.shape[1]
    panel_terms = jnp.einsum(
        "gtf,gth->gfh",
        byrow.reshape(n_row, -1, slice_width),
        d_all.reshape(n_row, -1, unit_width),
        preferred_element_type=jnp.float32,
    )
    panel_rounded = lax.optimization_barrier(panel_terms.astype(jnp.bfloat16))
    w1_sum = jnp.sum(panel_rounded.astype(jnp.float32), axis=0)
    d_order = (
        d_all.reshape(n_row, n_col, tok_here, unit_width)
        .transpose(1, 0, 2, 3)
        .reshape(-1, unit_width)
    )
    slices = sum_at_owner(dot_last(d_order, w_in_e).astype(jnp.bfloat16), "col", 0)
    normed_gradient = lax.all_to_all(
        slices.astype(jnp.bfloat16), "row", split_axis=0, concat_axis=1, tiled=True
    ).astype(slices.dtype)
    grad_w_in = apply_mask(w1_sum.astype(jnp.bfloat16), mask_in)
    norm_gain_gradient = lax.psum(
        jnp.sum(normed_gradient * standardized_input, axis=0), ("row", "col")
    )
    gain_scaled = normed_gradient * layer_norm_gain[None, :]
    backward_result = inverse_deviation * (
        gain_scaled
        - jnp.mean(gain_scaled, axis=1, keepdims=True)
        - standardized_input * jnp.mean(gain_scaled * standardized_input, axis=1, keepdims=True)
    )
    grad_inputs = (out_grad.astype(jnp.float32) + backward_result).astype(jnp.bfloat16)
    return (output, grad_inputs, grad_w_in, grad_w_out, norm_gain_gradient)


def solution(mesh):
    in_specs = (
        P(("row", "col"), None),
        P(),
        P("row", "col"),
        P("col", "row"),
        P(),
        P(),
        P(("row", "col"), None),
    )
    out_specs = (
        P(("row", "col"), None),
        P(("row", "col"), None),
        P("row", "col"),
        P("col", "row"),
        P(),
    )
    return jax.shard_map(shards, mesh=mesh, in_specs=in_specs, out_specs=out_specs, check_vma=False)
```

profile of v0, /device:TPU:1, one launch (start us, length us, event | category | flops | bytes accessed | tf_op | source)
XLA Modules:
  0.0 768.9 jit_solution(16966023902262134158)
XLA Ops:
  7.2 0.0 all-gather.5.cloned.1.call-start
  7.2 1.1 convert_reduce_fusion.1
  8.3 1.2 fusion.27
  9.5 1.0 fusion.20
  10.5 10.9 %all_to_all.42 = bf16[8,4,2048]{2,0,1:T(8,128)(2,1)} all-to-all(bf16[8,4,2048]{2,0,1:T(8,128)(2,1)S(1)} %bitcast.58), channel_id=1, replica_groups=mesh['row'=4,'col'=32] {'row'}, dimensions={1} | all-to-all | bytes 262144 | tf_op jit(solution)/shard_map/all_to_all | solution.py:85
  21.4 0.0 all-gather.5.cloned.1.call-update
  21.4 0.0 all-gather.9.cloned.1.call-start
  21.5 0.7 all-gather.9.cloned.1.call-update
  22.2 0.0 reduce-scatter.3.cloned.1.call-start
  22.2 0.8 fusion.29
  23.0 0.1 dynamic_slice.6
  23.1 0.1 copy.31
  23.2 0.3 broadcast_in_dim.50
  23.5 0.6 copy.41
  24.2 1.2 copy.32
  25.4 132.9 %all-gather.5.cloned.1.call-done = bf16[1024,2048]{1,0:T(8,128)(2,1)} async-done(((bf16[32,2048]{1,0:T(8,128)(2,1)}), bf16[1024,2048]{1,0:T(8,128)(2,1)}) %all-gather.5.cloned.1.call-update) | async-done | bytes 4194320 | tf_op jit(solution)/shard_map/all_gather | solution.py:86
  158.2 0.0 copy-start.6
  158.2 2.6 copy.30
  160.9 0.2 copy-done.6
  161.1 3.4 convolution_convert_fusion.4
  164.4 0.0 reduce-scatter.3.cloned.1.call-update
  164.5 0.0 reduce-scatter.5.cloned.1.call-start
  164.5 152.4 %all-gather.9.cloned.1.call-done = bf16[256,8192]{1,0:T(8,128)(2,1)} async-done(((bf16[8,8192]{1,0:T(8,128)(2,1)}), bf16[256,8192]{1,0:T(8,128)(2,1)}) %all-gather.9.cloned.1.call-update) | async-done | bytes 4194320 | tf_op jit(solution)/shard_map/all_gather | solution.py:107
  316.9 55.4 %reduce-scatter.3.cloned.1.call-done = bf16[256,512]{1,0:T(8,128)(2,1)} async-done(((bf16[1024,512]{1,0:T(8,128)(2,1)}), bf16[256,512]{1,0:T(8,128)(2,1)}) %reduce-scatter.3.cloned.1.call-update) | async-done | bytes 262160 | tf_op jit(solution)/shard_map/reduce_scatter | solution.py:93
  372.3 8.0 %convolution_convert_fusion = bf16[512,8192]{1,0:T(8,128)(2,1)} fusion(bf16[256,8192]{1,0:T(8,128)(2,1)} %all-gather.9.cloned.1.call-done, bf16[256,512]{1,0:T(8,128)(2,1)} %reduce-scatter.3.cloned.1.call-done), kind=kOutput, calls=%fused_computation | convolution fusion | flops 2152988672 | bytes 12845056 | tf_op jit(solution)/shard_map/dot_general | solution.py:53
  380.4 0.0 reduce-scatter.5.cloned.1.call-update
  380.4 0.0 all-gather.7.cloned.1.call-start
  380.4 0.6 copy-done.5
  381.1 0.2 fusion.13
  381.3 0.1 dynamic_slice.7
  381.4 0.1 copy.33
  381.5 0.3 broadcast_in_dim.53
  381.8 0.6 copy.42
  382.5 75.6 %reduce-scatter.5.cloned.1.call-done = bf16[512,2048]{1,0:T(8,128)(2,1)} async-done(((bf16[512,8192]{1,0:T(8,128)(2,1)}), bf16[512,2048]{1,0:T(8,128)(2,1)}) %reduce-scatter.5.cloned.1.call-update) | async-done | bytes 2097168 | tf_op jit(solution)/shard_map/reduce_scatter | solution.py:110
  458.1 4.6 broadcast_select_fusion
  462.7 0.0 all-gather.7.cloned.1.call-update
  462.8 0.2 all-gather.11.cloned.1.call-start
  463.0 62.2 %all-gather.7.cloned.1.call-done = bf16[512,8192]{1,0:T(8,128)(2,1)} async-done(((bf16[512,2048]{1,0:T(8,128)(2,1)}), bf16[512,8192]{1,0:T(8,128)(2,1)}) %all-gather.7.cloned.1.call-update) | async-done | bytes 8388624 | tf_op jit(solution)/shard_map/all_gather | solution.py:100
  525.2 0.0 copy-done.4
  525.2 7.8 %fusion.3 = bf16[256,512]{1,0:T(8,128)(2,1)} fusion(bf16[512,8192]{1,0:T(8,128)(2,1)} %all-gather.7.cloned.1.call-done, bf16[256,8192]{1,0:T(8,128)(2,1)} %all-gather.9.cloned.1.call-done, bf16[256,512]{1,0:T(8,128)(2,1)S(1)} %copy-done.4), kind=kOutput, calls=%fused_computation.17 | convolution fusion | flops 2150105088 | bytes 13107200 | tf_op jit(solution)/shard_map/dot_general | solution.py:47
  533.1 0.0 all-gather.11.cloned.1.call-update
  533.1 20.3 %all-gather.11.cloned.1.call-done = bf16[1024,512]{1,0:T(8,128)(2,1)} async-done(((bf16[256,512]{1,0:T(8,128)(2,1)}), bf16[1024,512]{1,0:T(8,128)(2,1)}) %all-gather.11.cloned.1.call-update) | async-done | bytes 1048592 | tf_op jit(solution)/shard_map/all_gather | solution.py:117
  553.4 1.3 copy.35
  554.7 6.0 convolution_convert_fusion.3
  560.7 7.1 all-to-all-start.2
  567.8 7.7 %fusion = bf16[32,8,8192]{2,1,0:T(8,128)(2,1)} fusion(bf16[512,8192]{1,0:T(8,128)(2,1)} %all-gather.7.cloned.1.call-done, bf16[256,512]{1,0:T(8,128)(2,1)S(1)} %copy-done.4), kind=kOutput, calls=%fused_computation.2 | convolution fusion | flops 2150891520 | bytes 12845056 | tf_op jit(solution)/shard_map/dot_general | solution.py:102
  575.5 46.5 %all-to-all-done.2 = bf16[32,32,2048]{2,1,0:T(8,128)(2,1)} async-done(((bf16[32,32,2048]{2,1,0:T(8,128)(2,1)}), bf16[32,32,2048]{2,1,0:T(8,128)(2,1)}, u32[]{:S(2)}, u32[]{:S(2)}) %all-to-all-start.2) | async-done | bytes 4194336 | tf_op jit(solution)/shard_map/all_to_all | solution.py:18
  622.0 10.2 %all-to-all-start.1 = ((bf16[32,8,8192]{2,1,0:T(8,128)(2,1)}), bf16[32,8,8192]{2,1,0:T(8,128)(2,1)}, u32[]{:S(2)}, u32[]{:S(2)}) async-start(bf16[32,8,8192]{2,1,0:T(8,128)(2,1)} %fusion), calls=%async_computation.2 | async-start | bytes 8388608 | tf_op jit(solution)/shard_map/all_to_all | solution.py:18
  632.2 0.0 copy-done.2
  632.2 0.0 copy-done
  632.3 7.8 %convolution_convert_fusion.2 = bf16[4,2048,512]{2,1,0:T(8,128)(2,1)} fusion(bf16[4,256,512]{2,1,0:T(8,128)(2,1)S(1)} %bitcast.53, bf16[4,32,8,2048]{3,2,0,1:T(8,128)(2,1)} %bitcast.45), kind=kOutput, calls=%fused_computation.4 | convolution fusion | flops 2151677952 | bytes 13631488 | tf_op jit(solution)/shard_map/gtf,gth->gfh/dot_general | solution.py:119
  640.1 6.1 reduce_sum.84
  646.2 1.8 broadcast_select_fusion.2
  648.0 3.7 reduce_sum.81
  651.7 33.6 %all-to-all-done.1 = bf16[32,8,8192]{2,1,0:T(8,128)(2,1)} async-done(((bf16[32,8,8192]{2,1,0:T(8,128)(2,1)}), bf16[32,8,8192]{2,1,0:T(8,128)(2,1)}, u32[]{:S(2)}, u32[]{:S(2)}) %all-to-all-start.1) | async-done | bytes 4194336 | tf_op jit(solution)/shard_map/all_to_all | solution.py:18
  685.3 5.7 all-to-all-start.3
  691.0 2.8 convert_reduce_fusion
  693.8 2.3 all-to-all-done.3
  696.1 0.2 multiply_reduce_fusion
  696.3 0.0 copy-done.1
  696.3 0.3 fusion.26
  696.6 64.7 %psum.7 = f32[8192]{0:T(1024)} all-reduce(f32[8192]{0:T(1024)S(1)} %get-tuple-element.10), channel_id=1, replica_groups=mesh['row'=4,'col'=32] {'row','col'}, use_global_device_ids=true, to_apply=%region_12.13 | all-reduce | flops 8192 | bytes 65536 | tf_op jit(solution)/shard_map/psum | solution.py:137
  761.3 0.0 copy-done.3
  761.3 0.8 fusion.25
  (12 shorter events, 0.1 us)
Async XLA Ops:
  7.2 151.1 %all-gather.5.cloned.1.call-start = ((), (), s32[]{:S(2)}) async-start(), calls=%async_computation.6 | async-start | bytes 4325376 | tf_op jit(solution)/shard_map/all_gather | solution.py:86
  21.4 295.5 %all-gather.9.cloned.1.call-start = ((), (), s32[]{:S(2)}) async-start(), calls=%async_computation.9 | async-start | bytes 4325376 | tf_op jit(solution)/shard_map/all_gather | solution.py:107
  22.2 350.1 %reduce-scatter.3.cloned.1.call-start = ((), (), s32[]{:S(2)}) async-start(), calls=%async_computation.7 | async-start | bytes 1310720 | tf_op jit(solution)/shard_map/reduce_scatter | solution.py:93
  158.2 2.9 copy-start.6
  164.5 293.6 %reduce-scatter.5.cloned.1.call-start = ((), (), s32[]{:S(2)}) async-start(), calls=%async_computation.11 | async-start | bytes 10485760 | tf_op jit(solution)/shard_map/reduce_scatter | solution.py:110
  380.4 0.7 copy-start.5
  380.4 144.8 %all-gather.7.cloned.1.call-start = ((), (), s32[]{:S(2)}) async-start(), calls=%async_computation.8 | async-start | bytes 10485760 | tf_op jit(solution)/shard_map/all_gather | solution.py:100
  458.1 67.1 %copy-start.4 = (bf16[256,512]{1,0:T(8,128)(2,1)S(1)}, bf16[256,512]{1,0:T(8,128)(2,1)}, u32[]{:S(2)}) copy-start(bf16[256,512]{1,0:T(8,128)(2,1)} %reduce-scatter.3.cloned.1.call-done) | copy-start | bytes 786436
  462.8 90.6 %all-gather.11.cloned.1.call-start = ((), (), s32[]{:S(2)}) async-start(), calls=%async_computation.10 | async-start | bytes 1310720 | tf_op jit(solution)/shard_map/all_gather | solution.py:117
  560.7 61.4 %all-to-all-start.2 = ((bf16[32,32,2048]{2,1,0:T(8,128)(2,1)}), bf16[32,32,2048]{2,1,0:T(8,128)(2,1)}, u32[]{:S(2)}, u32[]{:S(2)}) async-start(bf16[32,32,2048]{2,1,0:T(8,128)(2,1)} %bitcast.47), calls=%async_computation.3 | async-start | bytes 8388608 | tf_op jit(solution)/shard_map/all_to_all | solution.py:18
  575.5 56.7 %copy-start.2 = (f32[8192]{0:T(1024)S(1)}, f32[8192]{0:T(1024)}, u32[]{:S(2)}) copy-start(f32[8192]{0:T(1024)} %param.8) | copy-start | bytes 98308
  575.5 56.7 %copy-start = (bf16[1024,512]{1,0:T(8,128)(2,1)S(1)}, bf16[1024,512]{1,0:T(8,128)(2,1)}, u32[]{:S(2)}) copy-start(bf16[1024,512]{1,0:T(8,128)(2,1)} %all-gather.11.cloned.1.call-done) | copy-start | bytes 3145732
  622.0 63.3 %all-to-all-start.1 = ((bf16[32,8,8192]{2,1,0:T(8,128)(2,1)}), bf16[32,8,8192]{2,1,0:T(8,128)(2,1)}, u32[]{:S(2)}, u32[]{:S(2)}) async-start(bf16[32,8,8192]{2,1,0:T(8,128)(2,1)} %fusion), calls=%async_computation.2 | async-start | bytes 8388608 | tf_op jit(solution)/shard_map/all_to_all | solution.py:18
  648.0 48.3 %copy-start.1 = (bf16[8,8192]{1,0:T(8,128)(2,1)S(1)}, bf16[8,8192]{1,0:T(8,128)(2,1)}, u32[]{:S(2)}) copy-start(bf16[8,8192]{1,0:T(8,128)(2,1)} %param.7) | copy-start | bytes 393220
  648.0 113.3 %copy-start.3 = (bf16[8,8192]{1,0:T(8,128)(2,1)S(1)}, bf16[8,8192]{1,0:T(8,128)(2,1)}, u32[]{:S(2)}) copy-start(bf16[8,8192]{1,0:T(8,128)(2,1)} %param.13) | copy-start | bytes 393220
  685.3 10.8 %all-to-all-start.3 = ((bf16[4,8,2048]{2,1,0:T(8,128)(2,1)}), bf16[4,8,2048]{2,1,0:T(8,128)(2,1)S(1)}, u32[]{:S(2)}, u32[]{:S(2)}) async-start(bf16[4,8,2048]{2,1,0:T(8,128)(2,1)} %bitcast.12), calls=%async_computation.4 | async-start | bytes 262144 | tf_op jit(solution)/shard_map/all_to_all | solution.py:133
Sparse Core Ops, SparseCore 0:
  21.6 136.6 all-gather.4
  159.9 157.0 all-gather.8
  320.1 52.1 reduce-scatter.2
  380.5 77.5 reduce-scatter.4
  462.9 62.2 all-gather.6
  533.2 20.1 all-gather.10
where the time goes:
time: 770 us; the launch traced here: 769 us
  waiting for transfers between devices  582 us (76%)
  blocking collectives  75.6 us (10%)
  matrix products  40.8 us (5%)
  other arithmetic  24.6 us (3%)
  starting transfers between devices  23.4 us (3%)
  between operations  14.2 us (2%)
  local copies, waits for them, and re-layouts  8.34 us (1%)
    all_gather x1, waiting for transfers between devices, shards(): grad_panel = lax.all_gather(out_grad, 'col', axis=0, tiled=True)  152 us
    all_gather x1, waiting for transfers between devices, shards(): allrows = lax.all_gather(swapped, 'col', axis=0, tiled=True)  133 us
    all_to_all x2, waiting for transfers between devices, sum_at_owner(): lax.all_to_all(pieces, axis, split_axis=0, concat_axis=0, tiled=True)  80.1 us
    reduce_scatter x1, waiting for transfers between devices, shards(): lax.psum_scatter(dot_first(activation, grad_panel).astype(jnp.bfloat16),...  75.6 us
    psum x1, blocking collectives, shards(): lax.psum(jnp.sum(normed_gradient * standardized_input, axis=0), ('row', '...  64.7 us
    all_gather x1, waiting for transfers between devices, shards(): w_out_full = lax.all_gather(w_out_e, 'row', axis=1, tiled=True)  62.2 us
    reduce_scatter x1, waiting for transfers between devices, shards(): lax.psum_scatter(jnp.dot(byrow, w_in_e, preferred_element_type=jnp.float3...  55.4 us
    all_gather x1, waiting for transfers between devices, shards(): d_all = lax.all_gather(d_pre, 'row', axis=0, tiled=True)  20.3 us
  transfers between devices with their start and end apart: 9, of which 9 were waited for; matrix products, arithmetic and copies ran while one was open for 5% of the time, Pallas kernels for 0%

commit v1 on v0

--- a/solution.py
+++ b/solution.py
@@ -135,7 +135,7 @@
     ).astype(slices.dtype)
     grad_w_in = apply_mask(w1_sum.astype(jnp.bfloat16), mask_in)
     norm_gain_gradient = lax.psum(
-        jnp.sum(normed_gradient * standardized_input, axis=0), ("row", "col")
+        lax.psum(jnp.sum(normed_gradient * standardized_input, axis=0), "col"), "row"
     )
     gain_scaled = normed_gradient * layer_norm_gain[None, :]
     backward_result = inverse_deviation * (

time: 770 us -> 874 us (1.14)
  blocking collectives: 75.6 us -> 180 us
    psum x1 -> x2, blocking collectives: 64.7 us -> 169 us  [the longest x1 128 us: shards(): lax.psum(jnp.sum(normed_gradient * standardized_input, axis=0), 'col')]
where the time goes in v1:
time: 874 us
  waiting for transfers between devices  582 us (67%)
  blocking collectives  180 us (21%)
  matrix products  40.8 us (5%)
  other arithmetic  24.6 us (3%)
  starting transfers between devices  23.4 us (3%)
  between operations  14.2 us (2%)
    all_gather x1, waiting for transfers between devices, shards(): grad_panel = lax.all_gather(out_grad, 'col', axis=0, tiled=True)  152 us
    all_gather x1, waiting for transfers between devices, shards(): allrows = lax.all_gather(swapped, 'col', axis=0, tiled=True)  133 us
    psum x1, blocking collectives, shards(): lax.psum(jnp.sum(normed_gradient * standardized_input, axis=0), 'col')  128 us
    all_to_all x2, waiting for transfers between devices, sum_at_owner(): lax.all_to_all(pieces, axis, split_axis=0, concat_axis=0, tiled=True)  80.1 us
    reduce_scatter x1, waiting for transfers between devices, shards(): lax.psum_scatter(dot_first(activation, grad_panel).astype(jnp.bfloat16),...  75.6 us
    all_gather x1, waiting for transfers between devices, shards(): w_out_full = lax.all_gather(w_out_e, 'row', axis=1, tiled=True)  62.2 us
    reduce_scatter x1, waiting for transfers between devices, shards(): lax.psum_scatter(jnp.dot(byrow, w_in_e, preferred_element_type=jnp.float3...  55.4 us
    psum x1, blocking collectives, shards(): lax.psum(lax.psum(jnp.sum(normed_gradient * standardized_input, axis=0),...  41.7 us
  transfers between devices with their start and end apart: 9, of which 9 were waited for; matrix products, arithmetic and copies ran while one was open for 5% of the time, Pallas kernels for 0%

profile of v1, /device:TPU:1, one launch (start us, length us, event | category | flops | bytes accessed | tf_op | source)
XLA Modules:
  0.0 873.6 jit_solution(6108246785835649484)
XLA Ops:
  7.2 0.0 all-gather.5.cloned.1.call-start
  7.2 1.1 convert_reduce_fusion.1
  8.3 1.2 fusion.27
  9.5 1.0 fusion.20
  10.5 10.9 %all_to_all.42 = bf16[8,4,2048]{2,0,1:T(8,128)(2,1)} all-to-all(bf16[8,4,2048]{2,0,1:T(8,128)(2,1)S(1)} %bitcast.58), channel_id=1, replica_groups=mesh['row'=4,'col'=32] {'row'}, dimensions={1} | all-to-all | bytes 262144 | tf_op jit(solution)/shard_map/all_to_all | solution.py:85
  21.4 0.0 all-gather.5.cloned.1.call-update
  21.4 0.0 all-gather.9.cloned.1.call-start
  21.5 0.7 all-gather.9.cloned.1.call-update
  22.2 0.0 reduce-scatter.3.cloned.1.call-start
  22.2 0.8 fusion.29
  23.0 0.1 dynamic_slice.6
  23.1 0.1 copy.31
  23.2 0.3 broadcast_in_dim.50
  23.5 0.6 copy.41
  24.2 1.2 copy.32
  25.4 132.9 %all-gather.5.cloned.1.call-done = bf16[1024,2048]{1,0:T(8,128)(2,1)} async-done(((bf16[32,2048]{1,0:T(8,128)(2,1)}), bf16[1024,2048]{1,0:T(8,128)(2,1)}) %all-gather.5.cloned.1.call-update) | async-done | bytes 4194320 | tf_op jit(solution)/shard_map/all_gather | solution.py:86
  158.2 2.6 copy.30
  160.9 0.2 copy-done.6
  161.1 3.4 convolution_convert_fusion.4
  164.4 0.0 reduce-scatter.3.cloned.1.call-update
  164.5 0.0 reduce-scatter.5.cloned.1.call-start
  164.5 152.4 %all-gather.9.cloned.1.call-done = bf16[256,8192]{1,0:T(8,128)(2,1)} async-done(((bf16[8,8192]{1,0:T(8,128)(2,1)}), bf16[256,8192]{1,0:T(8,128)(2,1)}) %all-gather.9.cloned.1.call-update) | async-done | bytes 4194320 | tf_op jit(solution)/shard_map/all_gather | solution.py:107
  316.9 55.4 %reduce-scatter.3.cloned.1.call-done = bf16[256,512]{1,0:T(8,128)(2,1)} async-done(((bf16[1024,512]{1,0:T(8,128)(2,1)}), bf16[256,512]{1,0:T(8,128)(2,1)}) %reduce-scatter.3.cloned.1.call-update) | async-done | bytes 262160 | tf_op jit(solution)/shard_map/reduce_scatter | solution.py:93
  372.3 8.0 convolution_convert_fusion
  380.4 0.0 reduce-scatter.5.cloned.1.call-update
  380.4 0.0 all-gather.7.cloned.1.call-start
  380.4 0.6 copy-done.5
  381.1 0.2 fusion.13
  381.3 0.1 dynamic_slice.7
  381.4 0.1 copy.33
  381.5 0.3 broadcast_in_dim.53
  381.8 0.6 copy.42
  382.5 75.6 %reduce-scatter.5.cloned.1.call-done = bf16[512,2048]{1,0:T(8,128)(2,1)} async-done(((bf16[512,8192]{1,0:T(8,128)(2,1)}), bf16[512,2048]{1,0:T(8,128)(2,1)}) %reduce-scatter.5.cloned.1.call-update) | async-done | bytes 2097168 | tf_op jit(solution)/shard_map/reduce_scatter | solution.py:110
  458.1 4.6 broadcast_select_fusion
  462.7 0.0 all-gather.7.cloned.1.call-update
  462.8 0.2 all-gather.11.cloned.1.call-start
  463.0 62.2 %all-gather.7.cloned.1.call-done = bf16[512,8192]{1,0:T(8,128)(2,1)} async-done(((bf16[512,2048]{1,0:T(8,128)(2,1)}), bf16[512,8192]{1,0:T(8,128)(2,1)}) %all-gather.7.cloned.1.call-update) | async-done | bytes 8388624 | tf_op jit(solution)/shard_map/all_gather | solution.py:100
  525.2 0.0 copy-done.4
  525.2 7.8 fusion.3
  533.1 0.0 all-gather.11.cloned.1.call-update
  533.1 20.3 %all-gather.11.cloned.1.call-done = bf16[1024,512]{1,0:T(8,128)(2,1)} async-done(((bf16[256,512]{1,0:T(8,128)(2,1)}), bf16[1024,512]{1,0:T(8,128)(2,1)}) %all-gather.11.cloned.1.call-update) | async-done | bytes 1048592 | tf_op jit(solution)/shard_map/all_gather | solution.py:117
  553.4 1.3 copy.35
  554.7 6.0 convolution_convert_fusion.3
  560.7 7.1 all-to-all-start.2
  567.8 7.7 fusion
  575.5 46.5 %all-to-all-done.2 = bf16[32,32,2048]{2,1,0:T(8,128)(2,1)} async-done(((bf16[32,32,2048]{2,1,0:T(8,128)(2,1)}), bf16[32,32,2048]{2,1,0:T(8,128)(2,1)}, u32[]{:S(2)}, u32[]{:S(2)}) %all-to-all-start.2) | async-done | bytes 4194336 | tf_op jit(solution)/shard_map/all_to_all | solution.py:18
  622.0 10.2 %all-to-all-start.1 = ((bf16[32,8,8192]{2,1,0:T(8,128)(2,1)}), bf16[32,8,8192]{2,1,0:T(8,128)(2,1)}, u32[]{:S(2)}, u32[]{:S(2)}) async-start(bf16[32,8,8192]{2,1,0:T(8,128)(2,1)} %fusion), calls=%async_computation.2 | async-start | bytes 8388608 | tf_op jit(solution)/shard_map/all_to_all | solution.py:18
  632.2 0.0 copy-done.2
  632.2 0.0 copy-done
  632.3 7.8 convolution_convert_fusion.2
  640.1 6.1 reduce_sum.84
  646.2 1.8 broadcast_select_fusion.2
  648.0 3.7 reduce_sum.81
  651.7 33.6 %all-to-all-done.1 = bf16[32,8,8192]{2,1,0:T(8,128)(2,1)} async-done(((bf16[32,8,8192]{2,1,0:T(8,128)(2,1)}), bf16[32,8,8192]{2,1,0:T(8,128)(2,1)}, u32[]{:S(2)}, u32[]{:S(2)}) %all-to-all-start.1) | async-done | bytes 4194336 | tf_op jit(solution)/shard_map/all_to_all | solution.py:18
  685.3 5.7 all-to-all-start.3
  691.0 2.8 convert_reduce_fusion
  693.8 2.3 all-to-all-done.3
  696.1 0.2 multiply_reduce_fusion
  696.3 0.0 copy-done.1
  696.3 0.3 fusion.26
  696.6 127.6 %psum.14 = f32[8192]{0:T(1024)S(1)} all-reduce(f32[8192]{0:T(1024)S(1)} %get-tuple-element.10), channel_id=1, replica_groups=mesh['row'=4,'col'=32] {'col'}, use_global_device_ids=true, to_apply=%region_12.13 | all-reduce | flops 8192 | bytes 65536 | tf_op jit(solution)/shard_map/psum | solution.py:138
  824.2 41.7 %psum.15 = f32[8192]{0:T(1024)} all-reduce(f32[8192]{0:T(1024)S(1)} %psum.14), channel_id=1, replica_groups=mesh['row'=4,'col'=32] {'row'}, use_global_device_ids=true, to_apply=%region_13.14 | all-reduce | flops 8192 | bytes 65536 | tf_op jit(solution)/shard_map/psum | solution.py:137
  865.9 0.0 copy-done.3
  865.9 0.8 fusion.25
  (13 shorter events, 0.1 us)
Async XLA Ops:
  7.2 151.1 %all-gather.5.cloned.1.call-start = ((), (), s32[]{:S(2)}) async-start(), calls=%async_computation.6 | async-start | bytes 4325376 | tf_op jit(solution)/shard_map/all_gather | solution.py:86
  21.4 295.5 %all-gather.9.cloned.1.call-start = ((), (), s32[]{:S(2)}) async-start(), calls=%async_computation.9 | async-start | bytes 4325376 | tf_op jit(solution)/shard_map/all_gather | solution.py:107
  22.2 350.1 %reduce-scatter.3.cloned.1.call-start = ((), (), s32[]{:S(2)}) async-start(), calls=%async_computation.7 | async-start | bytes 1310720 | tf_op jit(solution)/shard_map/reduce_scatter | solution.py:93
  158.2 2.9 copy-start.6
  164.5 293.6 %reduce-scatter.5.cloned.1.call-start = ((), (), s32[]{:S(2)}) async-start(), calls=%async_computation.11 | async-start | bytes 10485760 | tf_op jit(solution)/shard_map/reduce_scatter | solution.py:110
  380.4 0.7 copy-start.5
  380.4 144.8 %all-gather.7.cloned.1.call-start = ((), (), s32[]{:S(2)}) async-start(), calls=%async_computation.8 | async-start | bytes 10485760 | tf_op jit(solution)/shard_map/all_gather | solution.py:100
  458.1 67.1 %copy-start.4 = (bf16[256,512]{1,0:T(8,128)(2,1)S(1)}, bf16[256,512]{1,0:T(8,128)(2,1)}, u32[]{:S(2)}) copy-start(bf16[256,512]{1,0:T(8,128)(2,1)} %reduce-scatter.3.cloned.1.call-done) | copy-start | bytes 786436
  462.8 90.6 %all-gather.11.cloned.1.call-start = ((), (), s32[]{:S(2)}) async-start(), calls=%async_computation.10 | async-start | bytes 1310720 | tf_op jit(solution)/shard_map/all_gather | solution.py:117
  560.7 61.4 %all-to-all-start.2 = ((bf16[32,32,2048]{2,1,0:T(8,128)(2,1)}), bf16[32,32,2048]{2,1,0:T(8,128)(2,1)}, u32[]{:S(2)}, u32[]{:S(2)}) async-start(bf16[32,32,2048]{2,1,0:T(8,128)(2,1)} %bitcast.47), calls=%async_computation.3 | async-start | bytes 8388608 | tf_op jit(solution)/shard_map/all_to_all | solution.py:18
  575.5 56.7 %copy-start.2 = (f32[8192]{0:T(1024)S(1)}, f32[8192]{0:T(1024)}, u32[]{:S(2)}) copy-start(f32[8192]{0:T(1024)} %param.8) | copy-start | bytes 98308
  575.5 56.7 %copy-start = (bf16[1024,512]{1,0:T(8,128)(2,1)S(1)}, bf16[1024,512]{1,0:T(8,128)(2,1)}, u32[]{:S(2)}) copy-start(bf16[1024,512]{1,0:T(8,128)(2,1)} %all-gather.11.cloned.1.call-done) | copy-start | bytes 3145732
  622.0 63.3 %all-to-all-start.1 = ((bf16[32,8,8192]{2,1,0:T(8,128)(2,1)}), bf16[32,8,8192]{2,1,0:T(8,128)(2,1)}, u32[]{:S(2)}, u32[]{:S(2)}) async-start(bf16[32,8,8192]{2,1,0:T(8,128)(2,1)} %fusion), calls=%async_computation.2 | async-start | bytes 8388608 | tf_op jit(solution)/shard_map/all_to_all | solution.py:18
  648.0 48.3 %copy-start.1 = (bf16[8,8192]{1,0:T(8,128)(2,1)S(1)}, bf16[8,8192]{1,0:T(8,128)(2,1)}, u32[]{:S(2)}) copy-start(bf16[8,8192]{1,0:T(8,128)(2,1)} %param.7) | copy-start | bytes 393220
  648.0 217.9 %copy-start.3 = (bf16[8,8192]{1,0:T(8,128)(2,1)S(1)}, bf16[8,8192]{1,0:T(8,128)(2,1)}, u32[]{:S(2)}) copy-start(bf16[8,8192]{1,0:T(8,128)(2,1)} %param.13) | copy-start | bytes 393220
  685.3 10.8 %all-to-all-start.3 = ((bf16[4,8,2048]{2,1,0:T(8,128)(2,1)}), bf16[4,8,2048]{2,1,0:T(8,128)(2,1)S(1)}, u32[]{:S(2)}, u32[]{:S(2)}) async-start(bf16[4,8,2048]{2,1,0:T(8,128)(2,1)} %bitcast.12), calls=%async_computation.4 | async-start | bytes 262144 | tf_op jit(solution)/shard_map/all_to_all | solution.py:133
Sparse Core Ops, SparseCore 0:
  21.6 136.6 all-gather.4
  159.9 157.0 all-gather.8
  320.1 52.1 reduce-scatter.2
  380.5 77.5 reduce-scatter.4
  462.9 62.2 all-gather.6
  533.2 20.1 all-gather.10
